TPU v7x, 256 devices: a whole 4x4x8 slice. The times are simulated.
256 devices in a mesh: rows: 128 (over x, y_hi, z, core), cols: 2 (over y_lo).
Axes of the slice: x: 4, y: 4 (y_hi: 2, y_lo: 2; y = y_hi * 2 + y_lo), z: 8, core: 2. Of those that a mesh axis runs over, the one named last changes fastest.
Arguments:
- ancestor: bfloat16 [24576, 24576], P('rows', 'cols'), may hold values from -6 to 6
- panel_below: bfloat16 [2048, 512], P('rows'), may hold values from -0.0625 to 0.0625
- panel_beside: bfloat16 [2048, 512], P('rows'), may hold values from -0.0625 to 0.0625
- inverse_lower: bfloat16 [512, 512], replicated, may hold values from -3 to 3
- inverse_upper: bfloat16 [512, 512], replicated, may hold values from -3 to 3
- list_below: int32 [16], replicated, may hold values from 0 to 191, as said below
- list_beside: int32 [16], replicated, may hold values from 0 to 191, as said below
- second_below: bfloat16 [2048, 512], P('rows'), may hold values from -0.0625 to 0.0625
- second_beside: bfloat16 [2048, 512], P('rows'), may hold values from -0.0625 to 0.0625
- linked_below: bfloat16 [512, 512], replicated, may hold values from -0.0625 to 0.0625
- linked_beside: bfloat16 [512, 512], replicated, may hold values from -0.0625 to 0.0625
- second_lower: bfloat16 [512, 512], replicated, may hold values from -3 to 3
- second_upper: bfloat16 [512, 512], replicated, may hold values from -3 to 3
- blocks_below: int32 [16], replicated, may hold values from 0 to 191, as said below
- blocks_beside: int32 [16], replicated, may hold values from 0 to 191, as said below
Outputs:
- new_lower: bfloat16 [24576, 512], P('rows', 'cols')
- new_upper: bfloat16 [24576, 512], P(('cols', 'rows'))
- new_diagonal: bfloat16 [512, 512], P(None, 'cols')
- next_lower: bfloat16 [24576, 512], P('rows', 'cols')
- next_upper: bfloat16 [24576, 512], P(('cols', 'rows'))
- next_link: bfloat16 [512, 512], replicated
- next_diagonal: bfloat16 [512, 512], P(None, 'cols')
Inputs may be any that keep to these rules, and one draw needn't show every extreme that they name: `list_below`: 16 distinct block numbers in ascending order; block 0 and block 191 are always listed. `list_beside`: 16 distinct block numbers in ascending order; block 0 and block 191 are always listed. `blocks_below`: 16 distinct block numbers in ascending order; block 0 and block 191 are always listed. `blocks_beside`: 16 distinct block numbers in ascending order; block 0 and block 191 are always listed.
All inputs are finite; a program needn't handle non-finite values.
Results may differ from a plain program's by a relative error of at most 0.0077.
Values may be sent and summed in bfloat16 or wider, within the bound.
A program may use at most 128 MiB of HBM per device.

v0:
```python
import jax
import jax.numpy as jnp
from jax import lax
from jax.sharding import PartitionSpec as P

BLK = 128


def normalise(panel, inverse):
    return jnp.dot(panel, inverse, preferred_element_type=jnp.float32).astype(jnp.bfloat16)


def normalise_by_rows(panel, inverse):
    return lax.dot_general(
        panel, inverse, (((1,), (1,)), ((), ())), preferred_element_type=jnp.float32
    ).astype(jnp.bfloat16)


def inner_rows(left, right):
    return lax.dot_general(
        left, right, (((0,), (0,)), ((), ())), preferred_element_type=jnp.float32
    )


def own_half(panel, first_column, half_width):
    return lax.dynamic_slice_in_dim(panel, first_column, half_width, 1)


def listed_columns(tile, blocks, first_block):
    block_count = tile.shape[1] // BLK
    local_ids = blocks - first_block
    inside = jnp.logical_and(local_ids >= 0, local_ids < block_count)
    picked = jnp.take(
        tile.reshape(tile.shape[0], block_count, BLK),
        jnp.clip(local_ids, 0, block_count - 1),
        axis=1,
    )
    return (picked.reshape(tile.shape[0], blocks.shape[0] * BLK), jnp.repeat(inside, BLK))


def masked_product(picked, inside, panel):
    kept = jnp.where(inside[:, None], panel, jnp.zeros_like(panel))
    return jnp.dot(picked, kept, preferred_element_type=jnp.float32)


def listed_rows(strips, blocks):
    shaped = strips.reshape(strips.shape[0] // BLK, BLK, strips.shape[1])
    return jnp.take(shaped, blocks, axis=0).reshape(blocks.shape[0] * BLK, strips.shape[1])


def rows_onto(panel, blocks, first_row, row_count):
    global_rows = first_row + jnp.arange(row_count, dtype=jnp.int32)
    block_of = global_rows // BLK
    offset = global_rows % BLK
    matches = block_of[:, None] == blocks[None, :]
    position = jnp.sum(
        jnp.where(matches, jnp.arange(blocks.shape[0], dtype=jnp.int32)[None, :], 0), axis=1
    )
    present = jnp.any(matches, axis=1)
    picked = jnp.take(panel, position * BLK + offset, axis=0)
    return jnp.where(present[:, None], picked, jnp.zeros_like(picked))


def lower_block(partial_value):
    return (-lax.psum_scatter(partial_value, "cols", scatter_dimension=1, tiled=True)).astype(
        jnp.bfloat16
    )


def diag_block(base_value, picked_rows, lower_local):
    summed = lax.psum(inner_rows(picked_rows, lower_local), "rows")
    return (base_value - summed).astype(jnp.bfloat16)


def body(
    ancestor,
    panel_below,
    panel_beside,
    inverse_lower,
    inverse_upper,
    list_below,
    list_beside,
    second_below,
    second_beside,
    linked_below,
    linked_beside,
    second_lower,
    second_upper,
    blocks_below,
    blocks_beside,
):
    row_devices = lax.axis_size("rows")
    row_at = lax.axis_index("rows")
    col_at = lax.axis_index("cols")
    col_devices = lax.axis_size("cols")
    tile_rows = ancestor.shape[0]
    tile_cols = ancestor.shape[1]
    width = inverse_lower.shape[0]
    half_width = width // col_devices
    first_column = col_at * half_width
    unit_below = normalise(panel_below, inverse_lower)
    unit_beside = normalise_by_rows(panel_beside, inverse_upper)
    below_next = normalise(second_below, second_lower)
    beside_next = normalise_by_rows(second_beside, second_upper)
    unit_below, unit_beside, below_next, beside_next = (
        lax.all_gather(unit_below, "rows", axis=0, tiled=True),
        lax.all_gather(unit_beside, "rows", axis=0, tiled=True),
        lax.all_gather(below_next, "rows", axis=0, tiled=True),
        lax.all_gather(beside_next, "rows", axis=0, tiled=True),
    )
    strips = lax.all_to_all(ancestor, "rows", split_axis=1, concat_axis=0, tiled=True)
    strip_width = tile_cols // row_devices
    strip_start = (col_at * row_devices + row_at) * strip_width
    first_block = col_at * (tile_cols // BLK)
    row_start = row_at * tile_rows
    picked, inside = listed_columns(ancestor, list_below, first_block)
    new_lower = lower_block(masked_product(picked, inside, unit_below))
    new_upper = (-inner_rows(listed_rows(strips, list_beside), unit_beside)).astype(jnp.bfloat16)
    base_first = jnp.dot(
        inverse_upper,
        own_half(inverse_lower, first_column, half_width),
        preferred_element_type=jnp.float32,
    )
    new_diagonal = diag_block(
        base_first, rows_onto(unit_beside, list_beside, row_start, tile_rows), new_lower
    )
    link_below = normalise(linked_below, second_lower)
    link_beside = normalise_by_rows(linked_beside, second_upper)
    link_rows = lax.dynamic_slice_in_dim(link_below, first_column, half_width, 0)
    picked_next, inside_next = listed_columns(ancestor, blocks_below, first_block)
    partial_value = masked_product(picked_next, inside_next, below_next) + jnp.dot(
        new_lower, link_rows, preferred_element_type=jnp.float32
    )
    next_lower = lower_block(partial_value)
    first_row = (row_at == 0).astype(jnp.float32)
    link_term = inner_rows(
        new_upper, rows_onto(below_next, blocks_below, strip_start, strip_width)
    ) + first_row * jnp.dot(new_diagonal, link_rows, preferred_element_type=jnp.float32)
    next_link = (-lax.psum(link_term, ("rows", "cols"))).astype(jnp.bfloat16)
    next_upper = (
        -(
            inner_rows(listed_rows(strips, blocks_beside), beside_next)
            + jnp.dot(new_upper, link_beside, preferred_element_type=jnp.float32)
        )
    ).astype(jnp.bfloat16)
    base_second = jnp.dot(
        second_upper,
        own_half(second_lower, first_column, half_width),
        preferred_element_type=jnp.float32,
    ) - inner_rows(link_beside, own_half(next_link, first_column, half_width))
    next_diagonal = diag_block(
        base_second, rows_onto(beside_next, blocks_beside, row_start, tile_rows), next_lower
    )
    return (new_lower, new_upper, new_diagonal, next_lower, next_upper, next_link, next_diagonal)


def solution(mesh):
    return jax.shard_map(
        body,
        mesh=mesh,
        in_specs=(
            P("rows", "cols"),
            P("rows", None),
            P("rows", None),
            P(),
            P(),
            P(),
            P(),
            P("rows", None),
            P("rows", None),
            P(),
            P(),
            P(),
            P(),
            P(),
            P(),
        ),
        out_specs=(
            P("rows", "cols"),
            P(("cols", "rows"), None),
            P(None, "cols"),
            P("rows", "cols"),
            P(("cols", "rows"), None),
            P(),
            P(None, "cols"),
        ),
        check_vma=False,
    )
```

profile of v0, /device:TPU:2, one launch (start us, length us, event | category | flops | bytes accessed | tf_op | source)
XLA Modules:
  0.0 2101.3 jit_solution(3499471611282957993)
XLA Ops:
  7.2 1.9 convolution_convert_fusion.4
  9.2 1.5 convolution_convert_fusion.2
  11.5 5.8 copy_bitcast_fusion
  17.3 3.0 gather_fusion.1
  20.4 110.8 %all-gather.5.cloned.1.call-done = bf16[2048,512]{1,0:T(8,128)(2,1)} async-done(((bf16[16,512]{1,0:T(8,128)(2,1)}), bf16[2048,512]{1,0:T(8,128)(2,1)}) %all-gather.5.cloned.1.call-update) | async-done | bytes 2097168 | tf_op jit(solution)/shard_map/all_gather | solution.py:106
  131.3 3.1 fusion.2
  135.3 10.1 all_to_all.12
  145.3 9.5 copy.76
  154.8 9.5 all-to-all-start
  165.4 3.0 gather_fusion.4
  169.3 86.8 %all-gather.9.cloned.1.call-done = bf16[2048,512]{1,0:T(8,128)(2,1)} async-done(((bf16[16,512]{1,0:T(8,128)(2,1)}), bf16[2048,512]{1,0:T(8,128)(2,1)}) %all-gather.9.cloned.1.call-update) | async-done | bytes 2097168 | tf_op jit(solution)/shard_map/all_gather | solution.py:108
  256.1 2.2 fusion
  258.3 20.8 reduce-scatter.3.cloned.1.call-done
  281.6 120.8 %all-gather.11.cloned.1.call-done = bf16[2048,512]{1,0:T(8,128)(2,1)} async-done(((bf16[16,512]{1,0:T(8,128)(2,1)}), bf16[2048,512]{1,0:T(8,128)(2,1)}) %all-gather.11.cloned.1.call-update) | async-done | bytes 2097168 | tf_op jit(solution)/shard_map/all_gather | solution.py:109
  402.4 2.9 gather_fusion.6
  405.3 114.1 %all-gather.7.cloned.1.call-done = bf16[2048,512]{1,0:T(8,128)(2,1)} async-done(((bf16[16,512]{1,0:T(8,128)(2,1)}), bf16[2048,512]{1,0:T(8,128)(2,1)}) %all-gather.7.cloned.1.call-update) | async-done | bytes 2097168 | tf_op jit(solution)/shard_map/all_gather | solution.py:107
  519.4 2.9 gather_fusion.3
  523.5 13.4 reduce-scatter.5.cloned.1.call-done
  538.5 1.1 fusion.29
  540.8 1.5 convolution_convert_fusion
  542.3 3.3 gather_fusion
  545.6 1206.7 %all-reduce.6.cloned.1.call-done = (f32[512,256]{0,1:T(8,128)}, f32[512,256]{0,1:T(8,128)}) async-done(((f32[512,256]{0,1:T(8,128)}, f32[512,256]{0,1:T(8,128)}), (f32[512,256]{0,1:T(8,128)}, f32[512,256]{0,1:T(8,128)})) %all-reduce.6.cloned.1.call-update) | async-done | bytes 1048592 | tf_op jit(solution)/shard_map/psum | solution.py:71
  1752.3 1.4 fusion.10
  1754.6 1.3 convolution_multiply_fusion
  1755.9 8.2 copy.78
  1764.1 3.0 gather_fusion.2
  1767.1 1.3 fusion.12
  1769.0 1.3 convolution_add_fusion
  1770.4 3.0 gather_fusion.5
  1775.1 315.4 %all-reduce.4.cloned.1.call-done = f32[512,512]{1,0:T(8,128)} async-done(((f32[512,512]{1,0:T(8,128)}), f32[512,512]{1,0:T(8,128)}) %all-reduce.4.cloned.1.call-update) | async-done | bytes 1048592 | tf_op jit(solution)/shard_map/psum | solution.py:139
  2090.5 1.3 negate_convert_fusion
  2092.2 1.4 fusion.9
  (94 shorter events, 14.3 us)
Async XLA Ops:
  7.2 2.0 copy-start
  7.2 124.1 %all-gather.5.cloned.1.call-start = ((), (), s32[]{:S(2)}) async-start(), calls=%async_computation.3 | async-start | bytes 2113536 | tf_op jit(solution)/shard_map/all_gather | solution.py:106
  9.2 246.9 %all-gather.9.cloned.1.call-start = ((), (), s32[]{:S(2)}) async-start(), calls=%async_computation.6 | async-start | bytes 2113536 | tf_op jit(solution)/shard_map/all_gather | solution.py:108
  10.7 268.4 %reduce-scatter.3.cloned.1.call-start = ((), (), s32[]{:S(2)}) async-start(), calls=%async_computation.4 | async-start | bytes 589824 | tf_op jit(solution)/shard_map/reduce_scatter | solution.py:65
  131.2 3.1 copy-start.2
  131.2 3.1 copy-start.15
  134.3 268.1 %all-gather.11.cloned.1.call-start = ((), (), s32[]{:S(2)}) async-start(), calls=%async_computation.8 | async-start | bytes 2113536 | tf_op jit(solution)/shard_map/all_gather | solution.py:109
  154.8 9.6 copy-start.5
  154.8 9.6 copy-start.16
  154.8 1601.1 %all-to-all-start = ((bf16[192,128,96]{2,0,1:T(8,128)(2,1)}), bf16[192,128,96]{2,0,1:T(8,128)(2,1)}, u32[]{:S(2)}, u32[]{:S(2)}) async-start(bf16[192,128,96]{2,0,1:T(8,128)(2,1)} %copy.76), calls=%async_computation.1 | async-start | bytes 12582912 | tf_op jit(solution)/shard_map/all_to_all | solution.py:111
  164.3 4.2 copy-start.17
  164.3 4.2 copy-start.18
  164.3 4.3 copy-start.19
  164.3 4.5 copy-start.10
  164.3 355.1 %all-gather.7.cloned.1.call-start = ((), (), s32[]{:S(2)}) async-start(), calls=%async_computation.5 | async-start | bytes 2113536 | tf_op jit(solution)/shard_map/all_gather | solution.py:107
  165.3 371.6 %reduce-scatter.5.cloned.1.call-start = ((), (), s32[]{:S(2)}) async-start(), calls=%async_computation.7 | async-start | bytes 589824 | tf_op jit(solution)/shard_map/reduce_scatter | solution.py:65
  280.1 242.2 %copy-start.9 = (bf16[192,256]{1,0:T(8,128)(2,1)}, bf16[192,256]{1,0:T(8,128)(2,1)S(1)}, u32[]{:S(2)}) copy-start(bf16[192,256]{1,0:T(8,128)(2,1)S(1)} %negate_convert_fusion.2) | copy-start | bytes 294916
  281.1 1471.2 %all-reduce.6.cloned.1.call-start = ((), (), s32[]{:S(2)}) async-start(), calls=%async_computation.10 | async-start | bytes 2097152 | tf_op jit(solution)/shard_map/psum | solution.py:71
  537.8 0.6 copy-start.14
  538.5 1213.9 %copy-start.8 = (bf16[512,512]{1,0:T(8,128)(2,1)S(1)}, bf16[512,512]{1,0:T(8,128)(2,1)}, u32[]{:S(2)}) copy-start(bf16[512,512]{1,0:T(8,128)(2,1)} %param.24) | copy-start | bytes 1572868
  539.7 1550.8 %all-reduce.4.cloned.1.call-start = ((), (), s32[]{:S(2)}) async-start(), calls=%async_computation.9 | async-start | bytes 2097152 | tf_op jit(solution)/shard_map/psum | solution.py:139
  1755.9 11.2 copy-start.7
  1767.1 1.9 copy-start.4
  1767.1 1.9 copy-start.13
  1767.1 1.9 copy-start.20
  1768.4 0.6 copy-start.11
  1769.0 4.3 copy-start.1
  1773.4 0.9 copy-start.12
  1774.3 318.0 %copy-start.3 = (bf16[512,512]{1,0:T(8,128)(2,1)S(1)}, bf16[512,512]{1,0:T(8,128)(2,1)}, u32[]{:S(2)}) copy-start(bf16[512,512]{1,0:T(8,128)(2,1)} %param.33) | copy-start | bytes 1572868
  2091.8 2.6 copy-start.6
Sparse Core Ops, SparseCore 0:
  12.3 118.9 all-gather.4
  135.5 120.4 all-gather.8
  259.2 19.9 reduce-scatter.2
  283.3 119.0 all-gather.10
  406.5 112.8 all-gather.6
  521.7 15.1 reduce-scatter.4
  540.1 1212.1 all-reduce.5
  1770.5 319.9 all-reduce.3
where the time goes:
time: 2100 us
  waiting for transfers between devices  1990 us (95%)
  local copies, waits for them, and re-layouts  58.2 us (3%)
  matrix products  24.1 us (1%)
    psum x1, waiting for transfers between devices, diag_block(): summed = lax.psum(inner_rows(picked_rows, lower_local), 'rows')  1210 us
    psum x1, waiting for transfers between devices, body(): next_link = (-lax.psum(link_term, ('rows', 'cols'))).astype(jnp.bfloat16)  315 us
    all_gather x1, waiting for transfers between devices, body(): lax.all_gather(beside_next, 'rows', axis=0, tiled=True)  121 us
    all_gather x1, waiting for transfers between devices, body(): lax.all_gather(unit_beside, 'rows', axis=0, tiled=True)  114 us
    all_gather x1, waiting for transfers between devices, body(): lax.all_gather(unit_below, 'rows', axis=0, tiled=True)  111 us
    all_gather x1, waiting for transfers between devices, body(): lax.all_gather(below_next, 'rows', axis=0, tiled=True)  86.8 us
  transfers between devices with their start and end apart: 9, of which 8 were waited for; matrix products, arithmetic and copies ran while one was open for 3% of the time, Pallas kernels for 0%

commit v1 on v0

--- a/solution.py
+++ b/solution.py
@@ -103,7 +103,12 @@
     below_next = normalise(second_below, second_lower)
     beside_next = normalise_by_rows(second_beside, second_upper)
     unit_below, unit_beside, below_next, beside_next = (
-        lax.all_gather(unit_below, "rows", axis=0, tiled=True),
+        jnp.concatenate(
+            lax.all_to_all(
+                jnp.stack([unit_below for _ in range(lax.axis_size("rows"))]), "rows", 0, 0
+            ),
+            axis=0,
+        ),
         lax.all_gather(unit_beside, "rows", axis=0, tiled=True),
         lax.all_gather(below_next, "rows", axis=0, tiled=True),
         lax.all_gather(beside_next, "rows", axis=0, tiled=True),

time: 2100 us -> 1970 us (0.938)
  waiting for transfers between devices: 1990 us -> 1840 us
    all_gather x1 -> x0, waiting for transfers between devices: 111 us -> none  [body(): lax.all_gather(unit_below, 'rows', axis=0, tiled=True)]
    all_to_all x0 -> x1, waiting for transfers between devices: none -> 41.1 us  [body(): lax.all_to_all(jnp.stack([unit_below for _ in range(lax.axis_size('rows')...]
    all_gather x1, waiting for transfers between devices: 86.8 us -> 48.1 us  [body(): lax.all_gather(below_next, 'rows', axis=0, tiled=True)]
    reduce_scatter x2, waiting for transfers between devices: 34.3 us -> 0.03 us  [lower_block(): lax.psum_scatter(partial_value, 'cols', scatter_dimension=1, tiled=True)]
  transfers between devices with their start and end apart: 9 -> 9, of which waited for: 8 -> 6; matrix products, arithmetic and copies ran while one was open for 3% -> 3% of each run, Pallas kernels for 0% -> 0%
where the time goes in v1:
time: 1970 us
  waiting for transfers between devices  1840 us (93%)
  local copies, waits for them, and re-layouts  59.9 us (3%)
  starting transfers between devices  26.2 us (1%)
  matrix products  21.1 us (1%)
    psum x1, waiting for transfers between devices, diag_block(): summed = lax.psum(inner_rows(picked_rows, lower_local), 'rows')  1200 us
    psum x1, waiting for transfers between devices, body(): next_link = (-lax.psum(link_term, ('rows', 'cols'))).astype(jnp.bfloat16)  315 us
    all_gather x1, waiting for transfers between devices, body(): lax.all_gather(beside_next, 'rows', axis=0, tiled=True)  120 us
    all_gather x1, waiting for transfers between devices, body(): lax.all_gather(unit_beside, 'rows', axis=0, tiled=True)  114 us
    all_gather x1, waiting for transfers between devices, body(): lax.all_gather(below_next, 'rows', axis=0, tiled=True)  48.1 us
    all_to_all x1, waiting for transfers between devices, body(): lax.all_to_all(jnp.stack([unit_below for _ in range(lax.axis_size('rows')...  41.1 us
  transfers between devices with their start and end apart: 9, of which 6 were waited for; matrix products, arithmetic and copies ran while one was open for 3% of the time, Pallas kernels for 0%

profile of v1, /device:TPU:2, one launch (start us, length us, event | category | flops | bytes accessed | tf_op | source)
XLA Modules:
  0.0 1968.9 jit_solution(14450077130000370067)
XLA Ops:
  8.0 1.3 convolution_convert_fusion.4
  9.3 1.6 stack.2
  10.9 15.7 all-to-all-start
  27.8 5.8 copy_bitcast_fusion
  33.5 3.0 gather_fusion.1
  36.6 41.1 %all-to-all-done = bf16[128,16,512]{2,1,0:T(8,128)(2,1)S(1)} async-done(((bf16[128,16,512]{2,1,0:T(8,128)(2,1)}), bf16[128,16,512]{2,1,0:T(8,128)(2,1)S(1)}, u32[]{:S(2)}, u32[]{:S(2)}) %all-to-all-start) | async-done | bytes 2097184 | tf_op jit(solution)/shard_map/all_to_all | solution.py:107
  78.0 1.4 fusion.14
  80.3 10.1 all_to_all.16
  90.4 9.5 copy.76
  99.9 10.1 all-to-all-start.1
  111.2 3.0 gather_fusion.4
  115.1 48.1 %all-gather.6.cloned.1.call-done = bf16[2048,512]{1,0:T(8,128)(2,1)} async-done(((bf16[16,512]{1,0:T(8,128)(2,1)}), bf16[2048,512]{1,0:T(8,128)(2,1)}) %all-gather.6.cloned.1.call-update) | async-done | bytes 2097168 | tf_op jit(solution)/shard_map/all_gather | solution.py:113
  163.2 2.2 fusion
  167.7 119.9 %all-gather.8.cloned.1.call-done = bf16[2048,512]{1,0:T(8,128)(2,1)} async-done(((bf16[16,512]{1,0:T(8,128)(2,1)}), bf16[2048,512]{1,0:T(8,128)(2,1)}) %all-gather.8.cloned.1.call-update) | async-done | bytes 2097168 | tf_op jit(solution)/shard_map/all_gather | solution.py:114
  287.6 2.9 gather_fusion.6
  290.5 114.3 %all-gather.4.cloned.1.call-done = bf16[2048,512]{1,0:T(8,128)(2,1)} async-done(((bf16[16,512]{1,0:T(8,128)(2,1)}), bf16[2048,512]{1,0:T(8,128)(2,1)}) %all-gather.4.cloned.1.call-update) | async-done | bytes 2097168 | tf_op jit(solution)/shard_map/all_gather | solution.py:112
  404.7 2.9 gather_fusion.3
  407.7 1.1 fusion.27
  410.4 1.1 fusion.26
  412.7 1.5 convolution_convert_fusion
  414.2 3.3 gather_fusion
  417.5 1202.2 %all-reduce.6.cloned.1.call-done = (f32[512,256]{0,1:T(8,128)}, f32[512,256]{0,1:T(8,128)}) async-done(((f32[512,256]{0,1:T(8,128)}, f32[512,256]{0,1:T(8,128)}), (f32[512,256]{0,1:T(8,128)}, f32[512,256]{0,1:T(8,128)})) %all-reduce.6.cloned.1.call-update) | async-done | bytes 1048592 | tf_op jit(solution)/shard_map/psum | solution.py:71
  1619.7 1.4 fusion.7
  1622.0 1.3 convolution_multiply_fusion
  1623.3 8.2 copy.78
  1631.5 3.0 gather_fusion.2
  1634.5 1.3 fusion.9
  1636.4 1.3 convolution_add_fusion
  1637.8 3.0 gather_fusion.5
  1642.5 315.1 %all-reduce.4.cloned.1.call-done = f32[512,512]{1,0:T(8,128)} async-done(((f32[512,512]{1,0:T(8,128)}), f32[512,512]{1,0:T(8,128)}) %all-reduce.4.cloned.1.call-update) | async-done | bytes 1048592 | tf_op jit(solution)/shard_map/psum | solution.py:144
  1957.6 1.3 negate_convert_fusion
  1959.3 1.4 fusion.6
  (100 shorter events, 13.6 us)
Async XLA Ops:
  8.0 18.6 copy-start
  10.9 15.7 copy-start.15
  10.9 16.6 copy-start.20
  10.9 16.6 copy-start.21
  10.9 66.8 %all-to-all-start = ((bf16[128,16,512]{2,1,0:T(8,128)(2,1)}), bf16[128,16,512]{2,1,0:T(8,128)(2,1)S(1)}, u32[]{:S(2)}, u32[]{:S(2)}) async-start(bf16[128,16,512]{2,1,0:T(8,128)(2,1)} %stack.2), calls=%async_computation | async-start | bytes 4194304 | tf_op jit(solution)/shard_map/all_to_all | solution.py:107
  26.6 136.6 %all-gather.6.cloned.1.call-start = ((), (), s32[]{:S(2)}) async-start(), calls=%async_computation.6 | async-start | bytes 2113536 | tf_op jit(solution)/shard_map/all_gather | solution.py:113
  27.5 138.0 %reduce-scatter.3.cloned.1.call-start = ((), (), s32[]{:S(2)}) async-start(), calls=%async_computation.4 | async-start | bytes 589824 | tf_op jit(solution)/shard_map/reduce_scatter | solution.py:65
  77.9 1.5 copy-start.2
  77.9 1.5 copy-start.16
  79.4 208.2 %all-gather.8.cloned.1.call-start = ((), (), s32[]{:S(2)}) async-start(), calls=%async_computation.8 | async-start | bytes 2113536 | tf_op jit(solution)/shard_map/all_gather | solution.py:114
  99.9 10.2 copy-start.5
  99.9 10.2 copy-start.17
  99.9 1523.4 %all-to-all-start.1 = ((bf16[192,128,96]{2,0,1:T(8,128)(2,1)}), bf16[192,128,96]{2,0,1:T(8,128)(2,1)}, u32[]{:S(2)}, u32[]{:S(2)}) async-start(bf16[192,128,96]{2,0,1:T(8,128)(2,1)} %copy.76), calls=%async_computation.2 | async-start | bytes 12582912 | tf_op jit(solution)/shard_map/all_to_all | solution.py:116
  109.9 4.3 copy-start.18
  109.9 4.3 copy-start.19
  110.0 4.7 copy-start.10
  110.0 294.8 %all-gather.4.cloned.1.call-start = ((), (), s32[]{:S(2)}) async-start(), calls=%async_computation.5 | async-start | bytes 2113536 | tf_op jit(solution)/shard_map/all_gather | solution.py:112
  110.9 297.9 %reduce-scatter.5.cloned.1.call-start = ((), (), s32[]{:S(2)}) async-start(), calls=%async_computation.7 | async-start | bytes 589824 | tf_op jit(solution)/shard_map/reduce_scatter | solution.py:65
  166.4 241.2 %copy-start.9 = (bf16[192,256]{1,0:T(8,128)(2,1)}, bf16[192,256]{1,0:T(8,128)(2,1)S(1)}, u32[]{:S(2)}) copy-start(bf16[192,256]{1,0:T(8,128)(2,1)S(1)} %negate_convert_fusion.2) | copy-start | bytes 294916
  167.4 1452.3 %all-reduce.6.cloned.1.call-start = ((), (), s32[]{:S(2)}) async-start(), calls=%async_computation.10 | async-start | bytes 2097152 | tf_op jit(solution)/shard_map/psum | solution.py:71
  409.7 0.6 copy-start.14
  410.4 1209.4 %copy-start.8 = (bf16[512,512]{1,0:T(8,128)(2,1)S(1)}, bf16[512,512]{1,0:T(8,128)(2,1)}, u32[]{:S(2)}) copy-start(bf16[512,512]{1,0:T(8,128)(2,1)} %param.24) | copy-start | bytes 1572868
  411.6 1546.0 %all-reduce.4.cloned.1.call-start = ((), (), s32[]{:S(2)}) async-start(), calls=%async_computation.9 | async-start | bytes 2097152 | tf_op jit(solution)/shard_map/psum | solution.py:144
  1623.3 11.2 copy-start.7
  1634.5 1.9 copy-start.4
  1634.5 1.9 copy-start.13
  1634.5 1.9 copy-start.22
  1635.8 0.6 copy-start.11
  1636.4 4.3 copy-start.1
  1640.8 0.9 copy-start.12
  1641.7 317.6 %copy-start.3 = (bf16[512,512]{1,0:T(8,128)(2,1)S(1)}, bf16[512,512]{1,0:T(8,128)(2,1)}, u32[]{:S(2)}) copy-start(bf16[512,512]{1,0:T(8,128)(2,1)} %param.33) | copy-start | bytes 1572868
  1958.9 2.6 copy-start.6
Sparse Core Ops, SparseCore 0:
  31.7 131.4 all-gather.5
  167.5 120.0 all-gather.7
  291.9 112.8 all-gather.3
  411.7 1208.0 all-reduce.5
Sparse Core Ops, SparseCore 1:
  79.5 15.1 reduce-scatter.2
  167.5 17.3 reduce-scatter.4
  1637.9 319.7 all-reduce.3
